TPU v7x, 32 devices: a whole 2x2x4 slice. The times are simulated.
32 devices in a mesh: inputs: 8 (over z, y), tm: 4 (over x, core).
Axes of the slice: x: 2, y: 2, z: 4, core: 2. Of those that a mesh axis runs over, the one named last changes fastest.
Arguments:
- voltages: bfloat16 [128, 131072], P('inputs', 'tm'), may hold values from -8 to 8
- pfb_taps: float32 [8, 512], replicated, may hold values from -2 to 2
Outputs:
- visibilities: float32 [256, 1, 2, 128, 128], P(('inputs', 'tm'))
All inputs are finite; a program needn't handle non-finite values.
Results may differ from a plain program's by a relative error of at most 0.002.
Values may be sent and summed in bfloat16 or wider, within the bound.
No kernel may reach another device: no remote copies, remote signals or barrier semaphores. Data moves between devices by JAX's collectives and lax.ppermute only.
A program may use at most 128 MiB of HBM per device.

v0:
```python
import jax
import jax.numpy as jnp
from jax import lax
from jax.sharding import PartitionSpec as P

F = 256
TAPS = 8
TILE = 128
FRAME = 512


def from_behind(value, axis, steps):
    count = lax.axis_size(axis)
    initial, last = (max(0, -steps), min(count, count - steps))
    return lax.ppermute(value, axis, [(source, source + steps) for source in range(initial, last)])


def dft_table(chans, length):
    rows = jnp.arange(2 * chans, dtype=jnp.int32)
    freq = rows // 2
    part = rows % 2
    samp = jnp.arange(length, dtype=jnp.int32)
    phase = freq[:, None] * samp[None, :] % length
    angle = 2.0 * jnp.pi / length * phase.astype(jnp.float32)
    vals = jnp.where(part[:, None] == 0, jnp.cos(angle), -jnp.sin(angle))
    return (vals * (1.0 / length**0.5)).astype(jnp.bfloat16)


def tile_sums(spec, scale):
    left = jnp.concatenate([spec[:, 0], spec[:, 1]], axis=-1)
    twisted = jnp.concatenate([spec[:, 1], -spec[:, 0]], axis=-1)
    count_in = left.shape[1]
    blocks = count_in // TILE
    chans = left.shape[0]
    real_rows = []
    imag_rows = []
    for first in range(blocks):
        lower = first * TILE
        cols = left[:, lower:]
        real_part = jnp.einsum(
            "cik,cjk->cij", left[:, lower : lower + TILE], cols, preferred_element_type=jnp.float32
        )
        imag_part = jnp.einsum(
            "cik,cjk->cij",
            twisted[:, lower : lower + TILE],
            cols,
            preferred_element_type=jnp.float32,
        )
        count = blocks - first
        real_rows.append(real_part.reshape(chans, TILE, count, TILE).transpose(0, 2, 1, 3))
        imag_rows.append(imag_part.reshape(chans, TILE, count, TILE).transpose(0, 2, 1, 3))
    real_all = jnp.concatenate(real_rows, axis=1)
    imag_all = jnp.concatenate(imag_rows, axis=1)
    return jnp.stack([real_all, imag_all], axis=2) * scale


def on_device(voltages, pfb_taps):
    inp_local = voltages.shape[0]
    frames_local = voltages.shape[1] // FRAME
    previous = from_behind(voltages[:, voltages.shape[1] - (TAPS - 1) * FRAME :], "tm", 1)
    extended = jnp.concatenate([previous, voltages], axis=1).reshape(
        inp_local, frames_local + TAPS - 1, FRAME
    )
    filtered = jnp.zeros((inp_local, frames_local, FRAME), jnp.float32)
    for tap in range(TAPS):
        filtered = filtered + pfb_taps[tap][None, None, :] * extended[
            :, tap : tap + frames_local, :
        ].astype(jnp.float32)
    filtered = filtered.astype(jnp.bfloat16)
    table = dft_table(F, FRAME)
    spectra = jnp.einsum("kn,itn->kit", table, filtered, preferred_element_type=jnp.float32)
    spectra = spectra.astype(jnp.bfloat16).reshape(F, 2, inp_local, frames_local)
    blocks_time = lax.axis_size("tm")
    scale = 1.0 / (frames_local * blocks_time)
    turned = lax.all_to_all(
        lax.all_to_all(spectra, "inputs", split_axis=0, concat_axis=2, tiled=True),
        "tm",
        split_axis=0,
        concat_axis=3,
        tiled=True,
    )
    return tile_sums(turned, scale)


def solution(mesh):
    in_specs = (P("inputs", "tm"), P())
    out_specs = P(("inputs", "tm"), None, None, None, None)
    return jax.shard_map(
        on_device, mesh=mesh, in_specs=in_specs, out_specs=out_specs, check_vma=False
    )
```

profile of v0, /device:TPU:0, one launch (start us, length us, event | category | flops | bytes accessed | tf_op | source)
XLA Modules:
  0.0 76.3 jit_solution(17021184768935166234)
XLA Ops:
  0.0 0.9 %slice.60 = bf16[16,3584]{1,0:T(8,128)(2,1)S(1)} slice(bf16[16,32768]{1,0:T(8,128)(2,1)} %param.2), slice={[0:16], [29184:32768]} | slice | bytes 229376 | tf_op jit(solution)/shard_map/slice | solution.py:60
  0.9 2.4 %collective-permute-start = (bf16[16,3584]{1,0:T(8,128)(2,1)S(1)}, bf16[16,3584]{1,0:T(8,128)(2,1)S(1)}, u32[]{:S(2)}, u32[]{:S(2)}) collective-permute-start(bf16[16,3584]{1,0:T(8,128)(2,1)S(1)} %slice.60), channel_id=1, source_target_pairs={{0,1},{1,2},{2,3},{4,5},{5,6},{6,7},{8,9},{9,10},{10,11},{12,13},{... | collective-permute-start | bytes 344072 | tf_op jit(solution)/shard_map/ppermute | solution.py:15
  3.3 1.0 %fusion.32 = (f32[1,512]{1,0:T(1,128)S(1)}, f32[1,512]{1,0:T(1,128)S(1)}, f32[1,512]{1,0:T(1,128)S(1)}, f32[1,512]{1,0:T(1,128)S(1)}, f32[1,512]{1,0:T(1,128)S(1...) fusion(f32[8,512]{1,0:T(8,128)} %param.3), kind=kLoop, calls=%fused_computation.48 | loop fusion | bytes 32768 | tf_op jit(solution)/shard_map/slice | solution.py:66
  4.4 0.0 collective-permute-done
  4.4 1.3 %pad_maximum_fusion = bf16[16,36352]{1,0:T(8,128)(2,1)S(1)} fusion(bf16[16,32768]{1,0:T(8,128)(2,1)} %param.2, bf16[16,3584]{1,0:T(8,128)(2,1)S(1)} %collective-permute-done), kind=kLoop, calls=%fused_computation.7 | loop fusion | flops 2326528 | bytes 2326528 | tf_op jit(solution)/shard_map/concatenate | solution.py:61
  5.7 0.7 reshape.74
  6.4 6.5 %convolution_convert_fusion = bf16[512,16,64]{0,2,1:T(8,128)(2,1)S(1)} fusion(bf16[16,71,512]{2,1,0:T(8,128)(2,1)S(1)} %reshape.74, f32[512]{0:T(512)S(1)} %bitcast.42, f32[512]{0:T(512)S(1)} %bitcast.43, f32[512]{0:T(512)S(1)} %bitcast.37, f32[512]{0:T(512)S(1)} %bitcast.38, f32[512]{0:T(512)S(1)} %bitcast.39, f32[512]{0:T(512)S(1)} %bitcast.40, ...), kind=kOutput, calls=%fused_computation.4 | convolution fusion | flops 554696704 | bytes 9456128 | tf_op jit(solution)/shard_map/kn,itn->kit/dot_general | solution.py:71
  12.9 2.0 %copy.11 = bf16[512,16,64]{2,1,0:T(8,128)(2,1)S(1)} copy(bf16[512,16,64]{0,2,1:T(8,128)(2,1)S(1)} %convolution_convert_fusion) | data formatting | bytes 2097152 | tf_op jit(solution)/shard_map/convert_element_type | solution.py:72
  15.0 1.7 %reshape.77 = bf16[8,2,32768]{2,1,0:T(2,128)(2,1)S(1)} reshape(bf16[256,2,16,64]{3,2,1,0:T(8,128)(2,1)S(1)} %bitcast.27) | data formatting | bytes 2097152
  16.7 32.5 %all_to_all.36 = bf16[8,2,32768]{2,1,0:T(2,128)(2,1)} all-to-all(bf16[8,2,32768]{2,1,0:T(2,128)(2,1)S(1)} %reshape.77), channel_id=1, replica_groups=mesh['inputs'=8,'tm'=4] {'inputs'}, dimensions={0} | all-to-all | bytes 2097152 | tf_op jit(solution)/shard_map/all_to_all | solution.py:76
  49.1 3.1 %reshape.78 = bf16[256,2,16,64]{3,2,1,0:T(8,128)(2,1)S(1)} reshape(bf16[8,2,32768]{2,1,0:T(2,128)(2,1)} %all_to_all.36) | data formatting | bytes 2097152
  52.2 2.0 %copy.12 = bf16[8,32,2,16,64]{4,3,0,2,1:T(8,128)(2,1)} copy(bf16[8,32,2,16,64]{4,3,2,1,0:T(8,128)(2,1)S(1)} %bitcast.28) | data formatting | bytes 2097152 | tf_op jit(solution)/shard_map/all_to_all | solution.py:76
  54.2 2.0 %copy.13 = bf16[32,2,128,64]{2,3,1,0:T(8,128)(2,1)S(1)} copy(bf16[32,2,128,64]{3,2,1,0:T(8,128)(2,1)} %bitcast.29) | data formatting | bytes 2097152 | tf_op jit(solution)/shard_map/all_to_all | solution.py:76
  56.2 17.4 %all_to_all.37 = bf16[32,2,128,64]{2,3,1,0:T(8,128)(2,1)S(1)} all-to-all(bf16[32,2,128,64]{2,3,1,0:T(8,128)(2,1)S(1)} %copy.13), channel_id=1, replica_groups=mesh['inputs'=8,'tm'=4] {'tm'}, dimensions={0} | all-to-all | bytes 2097152 | tf_op jit(solution)/shard_map/all_to_all | solution.py:75
  73.6 0.1 copy.14
  73.7 0.1 fusion.31
  73.8 0.2 copy.19
  74.0 0.2 copy.18
  74.3 0.4 convolution_bitcast_fusion.1
  74.7 0.4 convolution_bitcast_fusion
  75.2 0.1 maximum_multiply_fusion
  75.3 1.1 %copy.17 = f32[8,1,2,128,128]{4,3,2,1,0:T(8,128)} copy(f32[8,1,2,128,128]{4,3,0,2,1:T(8,128)S(1)} %maximum_multiply_fusion) | data formatting | bytes 2097152 | tf_op jit(solution)/shard_map/mul | solution.py:54
  (3 shorter events, 0.0 us)
Async XLA Ops:
  0.9 3.5 %collective-permute-start = (bf16[16,3584]{1,0:T(8,128)(2,1)S(1)}, bf16[16,3584]{1,0:T(8,128)(2,1)S(1)}, u32[]{:S(2)}, u32[]{:S(2)}) collective-permute-start(bf16[16,3584]{1,0:T(8,128)(2,1)S(1)} %slice.60), channel_id=1, source_target_pairs={{0,1},{1,2},{2,3},{4,5},{5,6},{6,7},{8,9},{9,10},{10,11},{12,13},{... | collective-permute-start | bytes 344072 | tf_op jit(solution)/shard_map/ppermute | solution.py:15
where the time goes:
time: 76.7 us; the launch traced here: 76.3 us
  blocking collectives  49.9 us (65%)
  local copies, waits for them, and re-layouts  15.1 us (20%)
  matrix products  7.4 us (10%)
  starting transfers between devices  2.39 us (3%)
  other arithmetic  1.43 us (2%)
    all_to_all x1, blocking collectives, on_device(): lax.all_to_all(spectra, 'inputs', split_axis=0, concat_axis=2, tiled=True)  32.5 us
    all_to_all x1, blocking collectives, on_device(): lax.all_to_all(lax.all_to_all(spectra, 'inputs', split_axis=0, concat_axi...  17.4 us
    dot_general x1, matrix products, on_device(): jnp.einsum('kn,itn->kit', table, filtered, preferred_element_type=jnp.flo...  6.55 us
    unnamed x4, local copies, waits for them, and re-layouts  5.2 us
    all_to_all x2, local copies, waits for them, and re-layouts, on_device(): lax.all_to_all(spectra, 'inputs', split_axis=0, concat_axis=2, tiled=True)  3.96 us
    ppermute x1, starting transfers between devices, from_behind(): lax.ppermute(value, axis, [(source, source + steps) for source in range(i...  2.39 us
    convert_element_type x1, local copies, waits for them, and re-layouts, on_device(): spectra.astype(jnp.bfloat16).reshape(F, 2, inp_local, frames_local)  2.03 us
  transfers between devices with their start and end apart: 1, of which 0 were waited for; matrix products, arithmetic and copies ran while one was open for 1% of the time, Pallas kernels for 0%

commit v1 on v0

v1 whole, which is shorter than its diff:
```python
import functools, math
import jax
import jax.numpy as jnp
import numpy as np
from jax import lax
from jax.experimental import pallas as pl
from jax.experimental.pallas import tpu as pltpu
from jax.sharding import PartitionSpec as P

F = 256
TAPS = 8
TILE = 128
FRAME = 512
LANES = 128
GROUP = 8


def dft_table(chans, length):
    rows = np.arange(2 * chans)
    part, freq = rows // chans, rows % chans
    samp = np.arange(length)
    phase = freq[:, None] * samp[None, :] % length
    angle = np.float32(2.0 * np.pi / length) * phase.astype(np.float32)
    vals = np.where(part[:, None] == 0, np.cos(angle), -np.sin(angle))
    return jnp.asarray((vals * np.float32(1.0 / length**0.5)).astype(np.float32)).astype(jnp.bfloat16)


def front_kernel(halo_ref, volts_ref, taps_ref, table_ref, out_ref, filt_ref, filtb_ref, spec_ref):
    inp = volts_ref.shape[0]
    frames = volts_ref.shape[1] // FRAME
    chans = table_ref.shape[0] // 2
    nt = (((1,), (1,)), ((), ()))

    def group_of(slab, first, block):
        xs = [slab(g) for g in range(GROUP + TAPS - 1)]
        for t in range(GROUP):
            acc = None
            for tap in range(TAPS):
                term = taps_ref[tap : tap + 1, block : block + LANES] * xs[t + tap]
                acc = term if acc is None else acc + term
            filt_ref[block // LANES, pl.ds(first + t, inp, stride=frames), :] = acc

    for block in range(0, FRAME, LANES):

        def first_slab(g):
            if g < TAPS - 1:
                return halo_ref[:, g * FRAME + block : g * FRAME + block + LANES].astype(jnp.float32)
            at = (g - TAPS + 1) * FRAME + block
            return volts_ref[:, at : at + LANES].astype(jnp.float32)

        group_of(first_slab, 0, block)

        @pl.loop(1, frames // GROUP)
        def _(step):
            def slab(g):
                at = pl.multiple_of((step * GROUP + g - TAPS + 1) * FRAME + block, LANES)
                return volts_ref[:, pl.ds(at, LANES)].astype(jnp.float32)

            group_of(slab, step * GROUP, block)

    for block in range(0, FRAME, LANES):
        filtb_ref[:, block : block + LANES] = filt_ref[block // LANES].astype(jnp.bfloat16)
    low = lax.broadcasted_iota(jnp.int32, (chans, LANES), 1) < frames
    for pair in range(inp // 2):
        cols = filtb_ref[pair * 2 * frames : (pair + 1) * 2 * frames, :]
        both = lax.dot_general(table_ref[...], cols, nt, preferred_element_type=jnp.float32)
        real, imag = both[:chans], both[chans:]
        spec_ref[pl.ds(2 * pair, chans, stride=inp), :] = jnp.where(low, real, pltpu.roll(imag, frames, 1))
        spec_ref[pl.ds(2 * pair + 1, chans, stride=inp), :] = jnp.where(low, pltpu.roll(real, frames, 1), imag)
    out_ref[...] = spec_ref[...].astype(jnp.bfloat16)


def front(halo, volts, taps, table):
    inp = volts.shape[0]
    frames = volts.shape[1] // FRAME
    assert 2 * frames == LANES
    vmem = pl.BlockSpec(memory_space=pltpu.VMEM)
    return pl.pallas_call(
        front_kernel,
        out_shape=jax.ShapeDtypeStruct((F * inp, LANES), jnp.bfloat16),
        in_specs=[vmem] * 4,
        out_specs=vmem,
        scratch_shapes=[
            pltpu.VMEM((FRAME // LANES, inp * frames, LANES), jnp.float32),
            pltpu.VMEM((inp * frames, FRAME), jnp.bfloat16),
            pltpu.VMEM((F * inp, LANES), jnp.float32),
        ],
        name="front",
    )(halo, volts, taps, table)


def tiles_kernel(groups, blocks_time, scale, spec_ref, out_ref):
    inp = spec_ref.shape[2]
    per = TILE // inp
    half = LANES // 2
    nt = (((1,), (1,)), ((), ()))
    sign = jnp.where(lax.broadcasted_iota(jnp.int32, (TILE, LANES), 1) < half, 1.0, -1.0)

    def side(tile):
        cols = []
        for tm in range(blocks_time):
            cols.append(
                jnp.concatenate(
                    [spec_ref[(tile * per + g) * blocks_time + tm, 0] for g in range(per)], axis=0
                )
            )
        return cols

    sides = [side(tile) for tile in range(groups // per)]
    pair = 0
    for a in range(len(sides)):
        left = jnp.concatenate(sides[a], axis=1)
        twisted = jnp.concatenate(
            [(pltpu.roll(c.astype(jnp.float32), half, 1) * sign).astype(jnp.bfloat16) for c in sides[a]], axis=1
        )
        for b in range(a, len(sides)):
            right = jnp.concatenate(sides[b], axis=1)
            real = lax.dot_general(left, right, nt, preferred_element_type=jnp.float32)
            imag = lax.dot_general(twisted, right, nt, preferred_element_type=jnp.float32)
            out_ref[0, pair, 0] = real * scale
            out_ref[0, pair, 1] = imag * scale
            pair += 1


def tile_sums(spec, groups, blocks_time, scale):
    _, chans, inp, _ = spec.shape
    count = groups * inp // TILE
    pairs = count * (count + 1) // 2
    return pl.pallas_call(
        functools.partial(tiles_kernel, groups, blocks_time, scale),
        out_shape=jax.ShapeDtypeStruct((chans, pairs, 2, TILE, TILE), jnp.float32),
        grid=(chans,),
        in_specs=[pl.BlockSpec((groups * blocks_time, 1, inp, LANES), lambda c: (0, c, 0, 0))],
        out_specs=pl.BlockSpec((1, pairs, 2, TILE, TILE), lambda c: (c, 0, 0, 0, 0)),
        name="tiles",
    )(spec)


def on_device(voltages, pfb_taps):
    inp = voltages.shape[0]
    frames = voltages.shape[1] // FRAME
    groups, blocks_time = lax.axis_size("inputs"), lax.axis_size("tm")
    tail = voltages[:, voltages.shape[1] - (TAPS - 1) * FRAME :]
    halo = lax.ppermute(tail, "tm", [(i, i + 1) for i in range(blocks_time - 1)])
    spec = front(halo, voltages, pfb_taps, dft_table(F, FRAME))
    turned = lax.all_to_all(spec, ("inputs", "tm"), split_axis=0, concat_axis=0, tiled=True)
    scale = 1.0 / (frames * blocks_time)
    every = groups * blocks_time
    return tile_sums(turned.reshape(every, F // every, inp, LANES), groups, blocks_time, scale)


def solution(mesh):
    return jax.shard_map(
        on_device,
        mesh=mesh,
        in_specs=(P("inputs", "tm"), P()),
        out_specs=P(("inputs", "tm"), None, None, None, None),
        check_vma=False,
    )
```

time: 76.7 us -> 54.2 us (0.71)
  local copies, waits for them, and re-layouts: 15.1 us -> 1.54 us
  blocking collectives: 49.9 us -> 36.4 us
  Pallas kernels: 0 us -> 12.6 us
  matrix products: 7.4 us -> 0 us
  other arithmetic: 1.43 us -> 0 us
  waiting for transfers between devices: 0.01 us -> 0.94 us
    all_to_all x2 -> x1, blocking collectives: 49.9 us -> 36.4 us  [on_device(): lax.all_to_all(spec, ('inputs', 'tm'), split_axis=0, concat_axis=0, tiled...]
    pallas_call x0 -> x2, Pallas kernels: none -> 12.6 us  [the longest x1 6.39 us: front(): pl.pallas_call(front_kernel, out_shape=jax.ShapeDtypeStruct((F * inp, LAN...]
    dot_general x3 -> x0, matrix products: 7.4 us -> none  [the longest x1 6.55 us: on_device(): jnp.einsum('kn,itn->kit', table, filtered, preferred_element_type=jnp.flo...]
    unnamed x4 -> x2, local copies, waits for them, and re-layouts: 5.2 us -> 0.63 us
    all_to_all x3 -> x0, local copies, waits for them, and re-layouts: 4.05 us -> none  [the longest x2 3.96 us: on_device(): lax.all_to_all(spectra, 'inputs', split_axis=0, concat_axis=2, tiled=True)]
    convert_element_type x1 -> x0, local copies, waits for them, and re-layouts: 2.03 us -> none  [on_device(): spectra.astype(jnp.bfloat16).reshape(F, 2, inp_local, frames_local)]
    concatenate x1 -> x0, other arithmetic: 1.3 us -> none  [on_device(): jnp.concatenate([previous, voltages], axis=1)]
    slice x3 -> x1, local copies, waits for them, and re-layouts: 2.03 us -> 0.91 us  [on_device(): tail = voltages[:, voltages.shape[1] - (TAPS - 1) * FRAME:]]
  transfers between devices with their start and end apart: 1 -> 1, of which waited for: 0 -> 1; matrix products, arithmetic and copies ran while one was open for 1% -> 0% of each run, Pallas kernels for 0% -> 0%
where the time goes in v1:
time: 54.2 us; the launch traced here: 53.8 us
  blocking collectives  36.4 us (67%)
  Pallas kernels  12.6 us (23%)
  starting transfers between devices  2.39 us (4%)
  local copies, waits for them, and re-layouts  1.54 us (3%)
  waiting for transfers between devices  0.94 us (2%)
    all_to_all x1, blocking collectives, on_device(): lax.all_to_all(spec, ('inputs', 'tm'), split_axis=0, concat_axis=0, tiled...  36.4 us
    pallas_call x1, Pallas kernels, front(): pl.pallas_call(front_kernel, out_shape=jax.ShapeDtypeStruct((F * inp, LAN...  6.39 us
    pallas_call x1, Pallas kernels, tile_sums(): pl.pallas_call(functools.partial(tiles_kernel, groups, blocks_time, scale...  6.16 us
    ppermute x1, starting transfers between devices, on_device(): lax.ppermute(tail, 'tm', [(i, i + 1) for i in range(blocks_time - 1)])  2.39 us
  transfers between devices with their start and end apart: 1, of which 1 were waited for; matrix products, arithmetic and copies ran while one was open for 0% of the time, Pallas kernels for 0%

profile of v1, /device:TPU:0, one launch (start us, length us, event | category | flops | bytes accessed | tf_op | source)
XLA Modules:
  0.0 53.8 jit_solution(246000436337621021)
XLA Ops:
  0.0 0.9 %slice.3 = bf16[16,3584]{1,0:T(8,128)(2,1)S(1)} slice(bf16[16,32768]{1,0:T(8,128)(2,1)} %volts_ref.1), slice={[0:16], [29184:32768]} | slice | bytes 229376 | tf_op jit(solution)/shard_map/slice | solution.py:143
  0.9 2.4 %collective-permute-start = (bf16[16,3584]{1,0:T(8,128)(2,1)S(1)}, bf16[16,3584]{1,0:T(8,128)(2,1)S(1)}, u32[]{:S(2)}, u32[]{:S(2)}) collective-permute-start(bf16[16,3584]{1,0:T(8,128)(2,1)S(1)} %slice.3), channel_id=1, source_target_pairs={{0,1},{1,2},{2,3},{4,5},{5,6},{6,7},{8,9},{9,10},{10,11},{12,13},{... | collective-permute-start | bytes 344072 | tf_op jit(solution)/shard_map/ppermute | solution.py:144
  3.3 0.9 %collective-permute-done.halo_ref = bf16[16,3584]{1,0:T(8,128)(2,1)S(1)} collective-permute-done((bf16[16,3584]{1,0:T(8,128)(2,1)S(1)}, bf16[16,3584]{1,0:T(8,128)(2,1)S(1)}, u32[]{:S(2)}, u32[]{:S(2)}) %collective-permute-start) | collective-permute-done | bytes 114720 | tf_op jit(solution)/shard_map/ppermute | solution.py:144
  4.2 0.0 copy-start
  4.2 0.6 %copy-done = bf16[16,3584]{1,0:T(8,128)(2,1)} copy-done((bf16[16,3584]{1,0:T(8,128)(2,1)}, bf16[16,3584]{1,0:T(8,128)(2,1)S(1)}, u32[]{:S(2)}) %copy-start) | copy-done | bytes 114712
  4.9 6.4 %front.1 = bf16[4096,128]{1,0:T(8,128)(2,1)} custom-call(bf16[16,3584]{1,0:T(8,128)(2,1)} %copy-done, bf16[16,32768]{1,0:T(8,128)(2,1)} %volts_ref.1, f32[8,512]{1,0:T(8,128)} %taps_ref.1, bf16[512,512]{1,0:T(8,128)(2,1)} %constant.3.table_ref), custom_call_target="tpu_custom_call" | custom-call | tf_op jit(solution)/shard_map/front/pallas_call | solution.py:78
  11.3 36.4 %all_to_all.9 = bf16[32,128,128]{2,1,0:T(8,128)(2,1)} all-to-all(bf16[32,128,128]{2,1,0:T(8,128)(2,1)} %bitcast.2), channel_id=1, replica_groups=mesh['inputs'=8,'tm'=4] {'inputs','tm'}, dimensions={0} | all-to-all | bytes 2097152 | tf_op jit(solution)/shard_map/all_to_all | solution.py:146
  47.7 6.2 %tiles.1 = f32[8,1,2,128,128]{4,3,2,1,0:T(8,128)} custom-call(bf16[32,8,16,128]{3,2,1,0:T(8,128)(2,1)} %bitcast.3), custom_call_target="tpu_custom_call" | custom-call | tf_op jit(solution)/shard_map/tiles/pallas_call | solution.py:129
Async XLA Ops:
  0.9 3.3 %collective-permute-start = (bf16[16,3584]{1,0:T(8,128)(2,1)S(1)}, bf16[16,3584]{1,0:T(8,128)(2,1)S(1)}, u32[]{:S(2)}, u32[]{:S(2)}) collective-permute-start(bf16[16,3584]{1,0:T(8,128)(2,1)S(1)} %slice.3), channel_id=1, source_target_pairs={{0,1},{1,2},{2,3},{4,5},{5,6},{6,7},{8,9},{9,10},{10,11},{12,13},{... | collective-permute-start | bytes 344072 | tf_op jit(solution)/shard_map/ppermute | solution.py:144
  4.2 0.6 %copy-start = (bf16[16,3584]{1,0:T(8,128)(2,1)}, bf16[16,3584]{1,0:T(8,128)(2,1)S(1)}, u32[]{:S(2)}) copy-start(bf16[16,3584]{1,0:T(8,128)(2,1)S(1)} %collective-permute-done.halo_ref) | copy-start | bytes 344068

commit v2 on v1

v2 whole, which is shorter than its diff:
```python
import functools

import jax
import jax.numpy as jnp
import numpy as np
from jax import lax
from jax.experimental import pallas as pl
from jax.experimental.pallas import tpu as pltpu
from jax.sharding import PartitionSpec as P

F = 256
TAPS = 8
TILE = 128
FRAME = 512
LANES = 128
GROUP = 8
LEAD = 16
WIDE = 4
NT = (((1,), (1,)), ((), ()))
VMEM = pl.BlockSpec(memory_space=pltpu.VMEM)
ANY = pl.BlockSpec(memory_space=pl.ANY)


def params(mib):
    return pltpu.CompilerParams(vmem_limit_bytes=mib << 20)


def dft_table(chans, length):
    phase = np.arange(chans)[:, None] * np.arange(length)[None, :] % length
    angle = np.float32(2.0 * np.pi / length) * phase.astype(np.float32)
    both = np.concatenate([np.cos(angle), -np.sin(angle)]) * np.float32(1.0 / length**0.5)
    return jnp.asarray(both.astype(np.float32)).astype(jnp.bfloat16)


def filter_group(slab, first, block, taps_ref, filt_ref, pitch):
    xs = [slab(g) for g in range(GROUP + TAPS - 1)]
    for t in range(GROUP):
        acc = None
        for tap in range(TAPS):
            term = taps_ref[tap : tap + 1, block : block + LANES] * xs[t + tap]
            acc = term if acc is None else acc + term
        filt_ref[block // LANES, pl.ds(first + t, xs[0].shape[0], stride=pitch), :] = acc


def later_kernel(volts_ref, taps_ref, out_ref, filt_ref):
    inp, frames = volts_ref.shape[0], volts_ref.shape[1] // FRAME
    pitch = filt_ref.shape[1] // inp
    for block in range(0, FRAME, LANES):

        @pl.loop(LEAD // GROUP, frames // GROUP)
        def _(step):
            def slab(g):
                at = pl.multiple_of((step * GROUP + g - TAPS + 1) * FRAME + block, LANES)
                return volts_ref[:, pl.ds(at, LANES)].astype(jnp.float32)

            filter_group(slab, step * GROUP, block, taps_ref, filt_ref, pitch)

        for i in range(inp):
            out_ref[i * frames + LEAD : (i + 1) * frames, block : block + LANES] = filt_ref[
                block // LANES, i * pitch + LEAD : i * pitch + frames, :
            ].astype(jnp.bfloat16)


def later(volts, taps):
    inp, frames = volts.shape[0], volts.shape[1] // FRAME
    return pl.pallas_call(
        later_kernel,
        out_shape=jax.ShapeDtypeStruct((inp * frames, FRAME), jnp.bfloat16),
        in_specs=[VMEM, VMEM],
        out_specs=VMEM,
        scratch_shapes=[pltpu.VMEM((FRAME // LANES, inp * (frames + 8), LANES), jnp.float32)],
        compiler_params=params(12),
        cost_estimate=pl.CostEstimate(flops=16 * inp * frames * FRAME, bytes_accessed=1 << 21, transcendentals=0),
        name="later",
    )(volts, taps)


def transform(filtb_ref, table, out_ref, spec_ref, inp):
    frames = filtb_ref.shape[0] // inp
    chans = table.shape[0] // 2
    pitch = spec_ref.shape[0] // chans
    low = lax.broadcasted_iota(jnp.int32, (chans, LANES), 1) < frames
    for quad in range(0, inp, WIDE):
        cols = filtb_ref[quad * frames : (quad + WIDE) * frames, :]
        both = lax.dot_general(table, cols, NT, preferred_element_type=jnp.float32)
        for p in range(WIDE // 2):
            real, imag = (both[c * chans : (c + 1) * chans, p * LANES : (p + 1) * LANES] for c in (0, 1))
            at = quad + 2 * p
            spec_ref[pl.ds(at, chans, stride=pitch), :] = jnp.where(low, real, pltpu.roll(imag, frames, 1))
            spec_ref[pl.ds(at + 1, chans, stride=pitch), :] = jnp.where(low, pltpu.roll(real, frames, 1), imag)
    for k in range(chans):
        out_ref[k * inp : (k + 1) * inp, :] = spec_ref[k * pitch : k * pitch + inp, :].astype(jnp.bfloat16)


def front_kernel(later_ref, halo_ref, head_ref, taps_ref, table_ref, out_ref, filtb_ref, filt_ref, spec_ref, sem):
    inp = head_ref.shape[0]
    frames = filtb_ref.shape[0] // inp
    copy = pltpu.make_async_copy(later_ref, filtb_ref, sem)
    copy.start()
    for block in range(0, FRAME, LANES):
        for first in range(0, LEAD, GROUP):

            def slab(g):
                t = first + g - (TAPS - 1)
                ref, at = (halo_ref, t + TAPS - 1) if t < 0 else (head_ref, t)
                return ref[:, at * FRAME + block : at * FRAME + block + LANES].astype(jnp.float32)

            filter_group(slab, first, block, taps_ref, filt_ref, filt_ref.shape[1] // inp)
    copy.wait()
    pitch = filt_ref.shape[1] // inp
    for block in range(0, FRAME, LANES):
        for i in range(inp):
            filtb_ref[i * frames : i * frames + LEAD, block : block + LANES] = filt_ref[
                block // LANES, i * pitch : i * pitch + LEAD, :
            ].astype(jnp.bfloat16)
    transform(filtb_ref, table_ref[...], out_ref, spec_ref, inp)


def front(filtered, halo, volts, taps, table):
    inp = volts.shape[0]
    frames = volts.shape[1] // FRAME
    assert 2 * frames == LANES
    chans = table.shape[0] // 2
    return pl.pallas_call(
        front_kernel,
        grid=(1,),
        out_shape=jax.ShapeDtypeStruct((chans * inp, LANES), jnp.bfloat16),
        in_specs=[ANY, VMEM, pl.BlockSpec((inp, LEAD * FRAME), lambda i: (0, 0)), VMEM, VMEM],
        out_specs=VMEM,
        scratch_shapes=[
            pltpu.VMEM(filtered.shape, jnp.bfloat16),
            pltpu.VMEM((FRAME // LANES, inp * (LEAD + 8), LANES), jnp.float32),
            pltpu.VMEM((chans * (inp + 8), LANES), jnp.float32),
            pltpu.SemaphoreType.DMA,
        ],
        compiler_params=params(16),
        name="front",
    )(filtered, halo, volts, taps, table)


def tiles_kernel(groups, blocks_time, scale, spec_ref, out_ref):
    chan = pl.program_id(0)
    per = TILE // spec_ref.shape[2]
    half = LANES // 2
    sign = jnp.where(lax.broadcasted_iota(jnp.int32, (TILE, LANES), 1) < half, 1.0, -1.0)

    def side(tile):
        return [
            jnp.concatenate([spec_ref[(tile * per + g) * blocks_time + tm, chan] for g in range(per)], axis=0)
            for tm in range(blocks_time)
        ]

    pair = 0
    for a in range(groups // per):
        cols = side(a)
        left = jnp.concatenate(cols, axis=1)
        twisted = jnp.concatenate(
            [(pltpu.roll(c.astype(jnp.float32), half, 1) * sign).astype(jnp.bfloat16) for c in cols], axis=1
        )
        for b in range(a, groups // per):
            right = left if b == a else jnp.concatenate(side(b), axis=1)
            out_ref[0, pair, 0] = lax.dot_general(left, right, NT, preferred_element_type=jnp.float32) * scale
            out_ref[0, pair, 1] = lax.dot_general(twisted, right, NT, preferred_element_type=jnp.float32) * scale
            pair += 1


def tile_sums(spec, groups, blocks_time, scale):
    _, chans, inp, _ = spec.shape
    count = groups * inp // TILE
    pairs = count * (count + 1) // 2
    return pl.pallas_call(
        functools.partial(tiles_kernel, groups, blocks_time, scale),
        out_shape=jax.ShapeDtypeStruct((chans, pairs, 2, TILE, TILE), jnp.float32),
        grid=(chans,),
        in_specs=[pl.BlockSpec(spec.shape, lambda c: (0, 0, 0, 0))],
        out_specs=pl.BlockSpec((1, pairs, 2, TILE, TILE), lambda c: (c, 0, 0, 0, 0)),
        compiler_params=params(32),
        name="tiles",
    )(spec)


def on_device(voltages, pfb_taps):
    inp = voltages.shape[0]
    frames = voltages.shape[1] // FRAME
    groups, blocks_time = lax.axis_size("inputs"), lax.axis_size("tm")
    tail = voltages[:, voltages.shape[1] - (TAPS - 1) * FRAME :]
    halo = lax.ppermute(tail, "tm", [(i, i + 1) for i in range(blocks_time - 1)])
    filtered = later(voltages, pfb_taps)
    spec = front(filtered, halo, voltages, pfb_taps, dft_table(F, FRAME))
    turned = lax.all_to_all(spec, ("inputs", "tm"), split_axis=0, concat_axis=0, tiled=True)
    scale = 1.0 / (frames * blocks_time)
    every = groups * blocks_time
    return tile_sums(turned.reshape(every, F // every, inp, LANES), groups, blocks_time, scale)


def solution(mesh):
    return jax.shard_map(
        on_device,
        mesh=mesh,
        in_specs=(P("inputs", "tm"), P()),
        out_specs=P(("inputs", "tm"), None, None, None, None),
        check_vma=False,
    )
```

time: 54.2 us -> 46 us (0.85)
  Pallas kernels: 12.6 us -> 6.61 us
  blocking collectives: 36.4 us -> 34.4 us
  waiting for transfers between devices: 0.94 us -> 0.01 us
  local copies, waits for them, and re-layouts: 1.54 us -> 2.23 us
    pallas_call x1 -> x2, Pallas kernels: 6.39 us -> 2.68 us  [the longest x1 1.44 us: front(): pl.pallas_call(front_kernel, grid=(1,), out_shape=jax.ShapeDtypeStruct((c...]
    pallas_call x1, Pallas kernels: 6.16 us -> 3.93 us  [tile_sums(): pl.pallas_call(functools.partial(tiles_kernel, groups, blocks_time, scale...]
    all_to_all x1, blocking collectives: 36.4 us -> 34.4 us  [on_device(): lax.all_to_all(spec, ('inputs', 'tm'), split_axis=0, concat_axis=0, tiled...]
    ppermute x1, waiting for transfers between devices: 0.94 us -> 0.01 us  [on_device(): lax.ppermute(tail, 'tm', [(i, i + 1) for i in range(blocks_time - 1)])]
    unnamed x2 -> x8, local copies, waits for them, and re-layouts: 0.63 us -> 1.31 us
  transfers between devices with their start and end apart: 1 -> 1, of which waited for: 1 -> 0; matrix products, arithmetic and copies ran while one was open for 0% -> 0% of each run, Pallas kernels for 0% -> 3%
where the time goes in v2:
time: 46 us; the launch traced here: 45.7 us
  blocking collectives  34.4 us (75%)
  Pallas kernels  6.61 us (14%)
  starting transfers between devices  2.39 us (5%)
  local copies, waits for them, and re-layouts  2.23 us (5%)
    all_to_all x1, blocking collectives, on_device(): lax.all_to_all(spec, ('inputs', 'tm'), split_axis=0, concat_axis=0, tiled...  34.4 us
    pallas_call x1, Pallas kernels, tile_sums(): pl.pallas_call(functools.partial(tiles_kernel, groups, blocks_time, scale...  3.93 us
    ppermute x1, starting transfers between devices, on_device(): lax.ppermute(tail, 'tm', [(i, i + 1) for i in range(blocks_time - 1)])  2.39 us
    pallas_call x1, Pallas kernels, front(): pl.pallas_call(front_kernel, grid=(1,), out_shape=jax.ShapeDtypeStruct((c...  1.44 us
    unnamed x8, local copies, waits for them, and re-layouts  1.31 us
    pallas_call x1, Pallas kernels, later(): pl.pallas_call(later_kernel, out_shape=jax.ShapeDtypeStruct((inp * frames...  1.24 us
  transfers between devices with their start and end apart: 1, of which 0 were waited for; matrix products, arithmetic and copies ran while one was open for 0% of the time, Pallas kernels for 3%

profile of v2, /device:TPU:0, one launch (start us, length us, event | category | flops | bytes accessed | tf_op | source)
XLA Modules:
  0.0 45.7 jit_solution(324604332491023957)
XLA Ops:
  0.0 0.0 copy-start.3
  0.0 0.9 %slice.3 = bf16[16,3584]{1,0:T(8,128)(2,1)S(1)} slice(bf16[16,32768]{1,0:T(8,128)(2,1)} %head_ref.1), slice={[0:16], [29184:32768]} | slice | bytes 229376 | tf_op jit(solution)/shard_map/slice | solution.py:186
  0.9 2.4 %collective-permute-start = (bf16[16,3584]{1,0:T(8,128)(2,1)S(1)}, bf16[16,3584]{1,0:T(8,128)(2,1)S(1)}, u32[]{:S(2)}, u32[]{:S(2)}) collective-permute-start(bf16[16,3584]{1,0:T(8,128)(2,1)S(1)} %slice.3), channel_id=1, source_target_pairs={{0,1},{1,2},{2,3},{4,5},{5,6},{6,7},{8,9},{9,10},{10,11},{12,13},{... | collective-permute-start | bytes 344072 | tf_op jit(solution)/shard_map/ppermute | solution.py:187
  3.3 0.0 copy-done.3
  3.3 0.0 copy-start
  3.3 1.2 %copy-done = bf16[16,32768]{1,0:T(8,128)(2,1)S(1)} copy-done((bf16[16,32768]{1,0:T(8,128)(2,1)S(1)}, bf16[16,32768]{1,0:T(8,128)(2,1)}, u32[]{:S(2)}) %copy-start) | copy-done | bytes 1048600
  4.6 0.0 copy-start.1
  4.6 0.0 copy-start.2
  4.6 1.2 %later.1.later_ref = bf16[1024,512]{1,0:T(8,128)(2,1)S(1)} custom-call(bf16[16,32768]{1,0:T(8,128)(2,1)S(1)} %copy-done, f32[8,512]{1,0:T(8,128)S(1)} %copy-done.3), custom_call_target="tpu_custom_call" | custom-call | flops 8388608 | bytes 2097152 | tf_op jit(solution)/shard_map/later/pallas_call | solution.py:66
  5.8 0.0 collective-permute-done.halo_ref
  5.8 0.0 copy-done.1
  5.8 0.1 copy-done.2
  5.9 1.4 %front.1 = bf16[4096,128]{1,0:T(8,128)(2,1)S(1)} custom-call(bf16[1024,512]{1,0:T(8,128)(2,1)S(1)} %later.1.later_ref, bf16[16,3584]{1,0:T(8,128)(2,1)S(1)} %collective-permute-done.halo_ref, bf16[16,32768]{1,0:T(8,128)(2,1)S(1)} %copy-done.1, f32[8,512]{1,0:T(8,128)S(1)} %copy-done.3, bf16[512,512]{1,0:T(8,128)(2,1)S(1)} %copy-done.2), custom_call_target="tpu_custom_call" | custom-call | tf_op jit(solution)/shard_map/front/pallas_call | solution.py:124
  7.4 34.4 %all_to_all.9 = bf16[32,128,128]{2,1,0:T(8,128)(2,1)S(1)} all-to-all(bf16[32,128,128]{2,1,0:T(8,128)(2,1)S(1)} %bitcast.3), channel_id=1, replica_groups=mesh['inputs'=8,'tm'=4] {'inputs','tm'}, dimensions={0} | all-to-all | bytes 2097152 | tf_op jit(solution)/shard_map/all_to_all | solution.py:190
  41.8 3.9 %tiles.1 = f32[8,1,2,128,128]{4,3,2,1,0:T(8,128)} custom-call(bf16[32,8,16,128]{3,2,1,0:T(8,128)(2,1)S(1)} %bitcast.2), custom_call_target="tpu_custom_call" | custom-call | tf_op jit(solution)/shard_map/tiles/pallas_call | solution.py:171
Async XLA Ops:
  0.0 3.3 %copy-start.3 = (f32[8,512]{1,0:T(8,128)S(1)}, f32[8,512]{1,0:T(8,128)}, u32[]{:S(2)}) copy-start(f32[8,512]{1,0:T(8,128)} %taps_ref.3) | copy-start | bytes 49156
  0.9 4.9 %collective-permute-start = (bf16[16,3584]{1,0:T(8,128)(2,1)S(1)}, bf16[16,3584]{1,0:T(8,128)(2,1)S(1)}, u32[]{:S(2)}, u32[]{:S(2)}) collective-permute-start(bf16[16,3584]{1,0:T(8,128)(2,1)S(1)} %slice.3), channel_id=1, source_target_pairs={{0,1},{1,2},{2,3},{4,5},{5,6},{6,7},{8,9},{9,10},{10,11},{12,13},{... | collective-permute-start | bytes 344072 | tf_op jit(solution)/shard_map/ppermute | solution.py:187
  3.3 1.2 %copy-start = (bf16[16,32768]{1,0:T(8,128)(2,1)S(1)}, bf16[16,32768]{1,0:T(8,128)(2,1)}, u32[]{:S(2)}) copy-start(bf16[16,32768]{1,0:T(8,128)(2,1)} %head_ref.1) | copy-start | bytes 3145732
  4.6 1.3 %copy-start.1 = (bf16[16,32768]{1,0:T(8,128)(2,1)S(1)}, bf16[16,32768]{1,0:T(8,128)(2,1)}, u32[]{:S(2)}) copy-start(bf16[16,32768]{1,0:T(8,128)(2,1)} %head_ref.1) | copy-start | bytes 3145732
  4.6 1.4 %copy-start.2 = (bf16[512,512]{1,0:T(8,128)(2,1)S(1)}, bf16[512,512]{1,0:T(8,128)(2,1)}, u32[]{:S(2)}) copy-start(bf16[512,512]{1,0:T(8,128)(2,1)} %constant.3.table_ref) | copy-start | bytes 1572868

commit v3 on v2

--- a/solution.py
+++ b/solution.py
@@ -40,6 +40,25 @@
             term = taps_ref[tap : tap + 1, block : block + LANES] * xs[t + tap]
             acc = term if acc is None else acc + term
         filt_ref[block // LANES, pl.ds(first + t, xs[0].shape[0], stride=pitch), :] = acc
+
+
+def tail_kernel(volts_ref, tail_ref, sem):
+    span = tail_ref.shape[1]
+    copy = pltpu.make_async_copy(volts_ref.at[:, pl.ds(volts_ref.shape[1] - span, span)], tail_ref, sem)
+    copy.start()
+    copy.wait()
+
+
+def last_frames(volts):
+    return pl.pallas_call(
+        tail_kernel,
+        out_shape=jax.ShapeDtypeStruct((volts.shape[0], (TAPS - 1) * FRAME), volts.dtype),
+        in_specs=[ANY],
+        out_specs=VMEM,
+        scratch_shapes=[pltpu.SemaphoreType.DMA],
+        compiler_params=params(62),
+        name="tail",
+    )(volts)
 
 
 def later_kernel(volts_ref, taps_ref, out_ref, filt_ref):
@@ -123,9 +142,8 @@
     chans = table.shape[0] // 2
     return pl.pallas_call(
         front_kernel,
-        grid=(1,),
         out_shape=jax.ShapeDtypeStruct((chans * inp, LANES), jnp.bfloat16),
-        in_specs=[ANY, VMEM, pl.BlockSpec((inp, LEAD * FRAME), lambda i: (0, 0)), VMEM, VMEM],
+        in_specs=[ANY, VMEM, VMEM, VMEM, VMEM],
         out_specs=VMEM,
         scratch_shapes=[
             pltpu.VMEM(filtered.shape, jnp.bfloat16),
@@ -172,7 +190,7 @@
         functools.partial(tiles_kernel, groups, blocks_time, scale),
         out_shape=jax.ShapeDtypeStruct((chans, pairs, 2, TILE, TILE), jnp.float32),
         grid=(chans,),
-        in_specs=[pl.BlockSpec(spec.shape, lambda c: (0, 0, 0, 0))],
+        in_specs=[VMEM],
         out_specs=pl.BlockSpec((1, pairs, 2, TILE, TILE), lambda c: (c, 0, 0, 0, 0)),
         compiler_params=params(32),
         name="tiles",
@@ -183,7 +201,7 @@
     inp = voltages.shape[0]
     frames = voltages.shape[1] // FRAME
     groups, blocks_time = lax.axis_size("inputs"), lax.axis_size("tm")
-    tail = voltages[:, voltages.shape[1] - (TAPS - 1) * FRAME :]
+    tail = last_frames(voltages)
     halo = lax.ppermute(tail, "tm", [(i, i + 1) for i in range(blocks_time - 1)])
     filtered = later(voltages, pfb_taps)
     spec = front(filtered, halo, voltages, pfb_taps, dft_table(F, FRAME))

time: 46 us -> 47 us (1.022)
  local copies, waits for them, and re-layouts: 2.23 us -> 0.01 us
  Pallas kernels: 6.61 us -> 8.24 us
  blocking collectives: 34.4 us -> 36 us
    pallas_call x1 -> x2, Pallas kernels: 1.44 us -> 3.06 us  [the longest x1 1.64 us: last_frames(): pl.pallas_call(tail_kernel, out_shape=jax.ShapeDtypeStruct((volts.shape[0...]
    all_to_all x1, blocking collectives: 34.4 us -> 36 us  [on_device(): lax.all_to_all(spec, ('inputs', 'tm'), split_axis=0, concat_axis=0, tiled...]
    unnamed x8 -> x6, local copies, waits for them, and re-layouts: 1.31 us -> 0.01 us
    slice x1 -> x0, local copies, waits for them, and re-layouts: 0.92 us -> none  [on_device(): tail = voltages[:, voltages.shape[1] - (TAPS - 1) * FRAME:]]
where the time goes in v3:
time: 47 us; the launch traced here: 46.8 us
  blocking collectives  36 us (77%)
  Pallas kernels  8.24 us (18%)
  starting transfers between devices  2.53 us (5%)
    all_to_all x1, blocking collectives, on_device(): lax.all_to_all(spec, ('inputs', 'tm'), split_axis=0, concat_axis=0, tiled...  36 us
    pallas_call x1, Pallas kernels, tile_sums(): pl.pallas_call(functools.partial(tiles_kernel, groups, blocks_time, scale...  3.93 us
    ppermute x1, starting transfers between devices, on_device(): lax.ppermute(tail, 'tm', [(i, i + 1) for i in range(blocks_time - 1)])  2.53 us
    pallas_call x1, Pallas kernels, last_frames(): pl.pallas_call(tail_kernel, out_shape=jax.ShapeDtypeStruct((volts.shape[0...  1.64 us
    pallas_call x1, Pallas kernels, front(): pl.pallas_call(front_kernel, out_shape=jax.ShapeDtypeStruct((chans * inp,...  1.42 us
    pallas_call x1, Pallas kernels, later(): pl.pallas_call(later_kernel, out_shape=jax.ShapeDtypeStruct((inp * frames...  1.25 us
  transfers between devices with their start and end apart: 1, of which 0 were waited for; matrix products, arithmetic and copies ran while one was open for 0% of the time, Pallas kernels for 3%

profile of v3, /device:TPU:0, one launch (start us, length us, event | category | flops | bytes accessed | tf_op | source)
XLA Modules:
  0.0 46.8 jit_solution(15503762979916600529)
XLA Ops:
  0.0 0.0 copy-start
  0.0 0.0 copy-start.2
  0.0 1.6 %tail.1 = bf16[16,3584]{1,0:T(8,128)(2,1)} custom-call(bf16[16,32768]{1,0:T(8,128)(2,1)} %head_ref.1), custom_call_target="tpu_custom_call" | custom-call | tf_op jit(solution)/shard_map/tail/pallas_call | solution.py:53
  1.7 0.0 copy-start.1
  1.7 2.5 %collective-permute-start = (bf16[16,3584]{1,0:T(8,128)(2,1)}, bf16[16,3584]{1,0:T(8,128)(2,1)S(1)}, u32[]{:S(2)}, u32[]{:S(2)}) collective-permute-start(bf16[16,3584]{1,0:T(8,128)(2,1)} %tail.1), channel_id=1, source_target_pairs={{0,1},{1,2},{2,3},{4,5},{5,6},{6,7},{8,9},{9,10},{10,11},{12,13},{... | collective-permute-start | bytes 344072 | tf_op jit(solution)/shard_map/ppermute | solution.py:205
  4.2 0.0 copy-done
  4.2 0.0 copy-done.2
  4.2 1.3 %later.1.later_ref = bf16[1024,512]{1,0:T(8,128)(2,1)S(1)} custom-call(bf16[16,32768]{1,0:T(8,128)(2,1)S(1)} %copy-done, f32[8,512]{1,0:T(8,128)S(1)} %copy-done.2), custom_call_target="tpu_custom_call" | custom-call | flops 8388608 | bytes 2097152 | tf_op jit(solution)/shard_map/later/pallas_call | solution.py:85
  5.5 0.0 collective-permute-done.halo_ref
  5.5 0.0 copy-done.1
  5.5 1.4 %front.1 = bf16[4096,128]{1,0:T(8,128)(2,1)S(1)} custom-call(bf16[1024,512]{1,0:T(8,128)(2,1)S(1)} %later.1.later_ref, bf16[16,3584]{1,0:T(8,128)(2,1)S(1)} %collective-permute-done.halo_ref, bf16[16,32768]{1,0:T(8,128)(2,1)S(1)} %copy-done, f32[8,512]{1,0:T(8,128)S(1)} %copy-done.2, bf16[512,512]{1,0:T(8,128)(2,1)S(1)} %copy-done.1), custom_call_target="tpu_custom_call" | custom-call | tf_op jit(solution)/shard_map/front/pallas_call | solution.py:143
  6.9 36.0 %all_to_all.9 = bf16[32,128,128]{2,1,0:T(8,128)(2,1)S(1)} all-to-all(bf16[32,128,128]{2,1,0:T(8,128)(2,1)S(1)} %bitcast.3), channel_id=1, replica_groups=mesh['inputs'=8,'tm'=4] {'inputs','tm'}, dimensions={0} | all-to-all | bytes 2097152 | tf_op jit(solution)/shard_map/all_to_all | solution.py:208
  42.9 3.9 %tiles.1 = f32[8,1,2,128,128]{4,3,2,1,0:T(8,128)} custom-call(bf16[32,8,16,128]{3,2,1,0:T(8,128)(2,1)S(1)} %bitcast.2), custom_call_target="tpu_custom_call" | custom-call | tf_op jit(solution)/shard_map/tiles/pallas_call | solution.py:189
Async XLA Ops:
  0.0 4.2 %copy-start = (bf16[16,32768]{1,0:T(8,128)(2,1)S(1)}, bf16[16,32768]{1,0:T(8,128)(2,1)}, u32[]{:S(2)}) copy-start(bf16[16,32768]{1,0:T(8,128)(2,1)} %head_ref.1) | copy-start | bytes 3145732
  0.0 4.2 %copy-start.2 = (f32[8,512]{1,0:T(8,128)S(1)}, f32[8,512]{1,0:T(8,128)}, u32[]{:S(2)}) copy-start(f32[8,512]{1,0:T(8,128)} %taps_ref.3) | copy-start | bytes 49156
  1.7 3.8 %copy-start.1 = (bf16[512,512]{1,0:T(8,128)(2,1)S(1)}, bf16[512,512]{1,0:T(8,128)(2,1)}, u32[]{:S(2)}) copy-start(bf16[512,512]{1,0:T(8,128)(2,1)} %constant.3.table_ref) | copy-start | bytes 1572868
  1.7 3.8 %collective-permute-start = (bf16[16,3584]{1,0:T(8,128)(2,1)}, bf16[16,3584]{1,0:T(8,128)(2,1)S(1)}, u32[]{:S(2)}, u32[]{:S(2)}) collective-permute-start(bf16[16,3584]{1,0:T(8,128)(2,1)} %tail.1), channel_id=1, source_target_pairs={{0,1},{1,2},{2,3},{4,5},{5,6},{6,7},{8,9},{9,10},{10,11},{12,13},{... | collective-permute-start | bytes 344072 | tf_op jit(solution)/shard_map/ppermute | solution.py:205

commit v4 on v2

--- a/solution.py
+++ b/solution.py
@@ -123,9 +123,8 @@
     chans = table.shape[0] // 2
     return pl.pallas_call(
         front_kernel,
-        grid=(1,),
         out_shape=jax.ShapeDtypeStruct((chans * inp, LANES), jnp.bfloat16),
-        in_specs=[ANY, VMEM, pl.BlockSpec((inp, LEAD * FRAME), lambda i: (0, 0)), VMEM, VMEM],
+        in_specs=[ANY, VMEM, VMEM, VMEM, VMEM],
         out_specs=VMEM,
         scratch_shapes=[
             pltpu.VMEM(filtered.shape, jnp.bfloat16),
@@ -138,42 +137,48 @@
     )(filtered, halo, volts, taps, table)
 
 
-def tiles_kernel(groups, blocks_time, scale, spec_ref, out_ref):
-    chan = pl.program_id(0)
+def tiles_kernel(groups, blocks_time, scale, spec_ref, out_ref, held_ref, sem):
     per = TILE // spec_ref.shape[2]
     half = LANES // 2
     sign = jnp.where(lax.broadcasted_iota(jnp.int32, (TILE, LANES), 1) < half, 1.0, -1.0)
-
-    def side(tile):
-        return [
-            jnp.concatenate([spec_ref[(tile * per + g) * blocks_time + tm, chan] for g in range(per)], axis=0)
-            for tm in range(blocks_time)
-        ]
-
-    pair = 0
-    for a in range(groups // per):
-        cols = side(a)
-        left = jnp.concatenate(cols, axis=1)
-        twisted = jnp.concatenate(
-            [(pltpu.roll(c.astype(jnp.float32), half, 1) * sign).astype(jnp.bfloat16) for c in cols], axis=1
-        )
-        for b in range(a, groups // per):
-            right = left if b == a else jnp.concatenate(side(b), axis=1)
-            out_ref[0, pair, 0] = lax.dot_general(left, right, NT, preferred_element_type=jnp.float32) * scale
-            out_ref[0, pair, 1] = lax.dot_general(twisted, right, NT, preferred_element_type=jnp.float32) * scale
-            pair += 1
+    copies = []
+    for chan in range(spec_ref.shape[1]):
+
+        def side(tile):
+            return [
+                jnp.concatenate([spec_ref[(tile * per + g) * blocks_time + tm, chan] for g in range(per)], axis=0)
+                for tm in range(blocks_time)
+            ]
+
+        pair = 0
+        for a in range(groups // per):
+            cols = side(a)
+            left = jnp.concatenate(cols, axis=1)
+            twisted = jnp.concatenate(
+                [(pltpu.roll(c.astype(jnp.float32), half, 1) * sign).astype(jnp.bfloat16) for c in cols], axis=1
+            )
+            for b in range(a, groups // per):
+                right = left if b == a else jnp.concatenate(side(b), axis=1)
+                for part, mine in enumerate((left, twisted)):
+                    sums = lax.dot_general(mine, right, NT, preferred_element_type=jnp.float32)
+                    held_ref[chan, pair, part] = sums * scale
+                pair += 1
+        copies.append(pltpu.make_async_copy(held_ref.at[chan], out_ref.at[chan], sem.at[chan]))
+        copies[-1].start()
+    for copy in copies:
+        copy.wait()
 
 
 def tile_sums(spec, groups, blocks_time, scale):
     _, chans, inp, _ = spec.shape
     count = groups * inp // TILE
-    pairs = count * (count + 1) // 2
+    shape = (chans, count * (count + 1) // 2, 2, TILE, TILE)
     return pl.pallas_call(
         functools.partial(tiles_kernel, groups, blocks_time, scale),
-        out_shape=jax.ShapeDtypeStruct((chans, pairs, 2, TILE, TILE), jnp.float32),
-        grid=(chans,),
-        in_specs=[pl.BlockSpec(spec.shape, lambda c: (0, 0, 0, 0))],
-        out_specs=pl.BlockSpec((1, pairs, 2, TILE, TILE), lambda c: (c, 0, 0, 0, 0)),
+        out_shape=jax.ShapeDtypeStruct(shape, jnp.float32),
+        in_specs=[VMEM],
+        out_specs=ANY,
+        scratch_shapes=[pltpu.VMEM(shape, jnp.float32), pltpu.SemaphoreType.DMA((chans,))],
         compiler_params=params(32),
         name="tiles",
     )(spec)

time: 46 us -> 43.5 us (0.946)
  Pallas kernels: 6.61 us -> 4.13 us
    pallas_call x1, Pallas kernels: 3.93 us -> 1.46 us  [tile_sums(): pl.pallas_call(functools.partial(tiles_kernel, groups, blocks_time, scale...]
where the time goes in v4:
time: 43.5 us; the launch traced here: 43.3 us
  blocking collectives  34.5 us (79%)
  Pallas kernels  4.13 us (9%)
  starting transfers between devices  2.39 us (5%)
  local copies, waits for them, and re-layouts  2.23 us (5%)
    all_to_all x1, blocking collectives, on_device(): lax.all_to_all(spec, ('inputs', 'tm'), split_axis=0, concat_axis=0, tiled...  34.5 us
    ppermute x1, starting transfers between devices, on_device(): lax.ppermute(tail, 'tm', [(i, i + 1) for i in range(blocks_time - 1)])  2.39 us
    pallas_call x1, Pallas kernels, tile_sums(): pl.pallas_call(functools.partial(tiles_kernel, groups, blocks_time, scale...  1.46 us
    pallas_call x1, Pallas kernels, front(): pl.pallas_call(front_kernel, out_shape=jax.ShapeDtypeStruct((chans * inp,...  1.42 us
    unnamed x8, local copies, waits for them, and re-layouts  1.31 us
    pallas_call x1, Pallas kernels, later(): pl.pallas_call(later_kernel, out_shape=jax.ShapeDtypeStruct((inp * frames...  1.24 us
    slice x1, local copies, waits for them, and re-layouts, on_device(): tail = voltages[:, voltages.shape[1] - (TAPS - 1) * FRAME:]  0.92 us
  transfers between devices with their start and end apart: 1, of which 0 were waited for; matrix products, arithmetic and copies ran while one was open for 0% of the time, Pallas kernels for 3%

profile of v4, /device:TPU:0, one launch (start us, length us, event | category | flops | bytes accessed | tf_op | source)
XLA Modules:
  0.0 43.3 jit_solution(1613641901339965715)
XLA Ops:
  0.0 0.0 copy-start.3
  0.0 0.9 %slice.3 = bf16[16,3584]{1,0:T(8,128)(2,1)S(1)} slice(bf16[16,32768]{1,0:T(8,128)(2,1)} %head_ref.1), slice={[0:16], [29184:32768]} | slice | bytes 229376 | tf_op jit(solution)/shard_map/slice | solution.py:191
  0.9 2.4 %collective-permute-start = (bf16[16,3584]{1,0:T(8,128)(2,1)S(1)}, bf16[16,3584]{1,0:T(8,128)(2,1)S(1)}, u32[]{:S(2)}, u32[]{:S(2)}) collective-permute-start(bf16[16,3584]{1,0:T(8,128)(2,1)S(1)} %slice.3), channel_id=1, source_target_pairs={{0,1},{1,2},{2,3},{4,5},{5,6},{6,7},{8,9},{9,10},{10,11},{12,13},{... | collective-permute-start | bytes 344072 | tf_op jit(solution)/shard_map/ppermute | solution.py:192
  3.3 0.0 copy-done.3
  3.3 0.0 copy-start
  3.3 1.2 %copy-done = bf16[16,32768]{1,0:T(8,128)(2,1)S(1)} copy-done((bf16[16,32768]{1,0:T(8,128)(2,1)S(1)}, bf16[16,32768]{1,0:T(8,128)(2,1)}, u32[]{:S(2)}) %copy-start) | copy-done | bytes 1048600
  4.6 0.0 copy-start.1
  4.6 0.0 copy-start.2
  4.6 1.2 %later.1.later_ref = bf16[1024,512]{1,0:T(8,128)(2,1)S(1)} custom-call(bf16[16,32768]{1,0:T(8,128)(2,1)S(1)} %copy-done, f32[8,512]{1,0:T(8,128)S(1)} %copy-done.3), custom_call_target="tpu_custom_call" | custom-call | flops 8388608 | bytes 2097152 | tf_op jit(solution)/shard_map/later/pallas_call | solution.py:66
  5.8 0.0 collective-permute-done.halo_ref
  5.8 0.0 copy-done.1
  5.8 0.1 copy-done.2
  5.9 1.4 %front.1 = bf16[4096,128]{1,0:T(8,128)(2,1)S(1)} custom-call(bf16[1024,512]{1,0:T(8,128)(2,1)S(1)} %later.1.later_ref, bf16[16,3584]{1,0:T(8,128)(2,1)S(1)} %collective-permute-done.halo_ref, bf16[16,32768]{1,0:T(8,128)(2,1)S(1)} %copy-done.1, f32[8,512]{1,0:T(8,128)S(1)} %copy-done.3, bf16[512,512]{1,0:T(8,128)(2,1)S(1)} %copy-done.2), custom_call_target="tpu_custom_call" | custom-call | tf_op jit(solution)/shard_map/front/pallas_call | solution.py:124
  7.3 34.5 %all_to_all.9 = bf16[32,128,128]{2,1,0:T(8,128)(2,1)S(1)} all-to-all(bf16[32,128,128]{2,1,0:T(8,128)(2,1)S(1)} %bitcast.3), channel_id=1, replica_groups=mesh['inputs'=8,'tm'=4] {'inputs','tm'}, dimensions={0} | all-to-all | bytes 2097152 | tf_op jit(solution)/shard_map/all_to_all | solution.py:195
  41.8 1.5 %tiles.1 = f32[8,1,2,128,128]{4,3,2,1,0:T(8,128)} custom-call(bf16[32,8,16,128]{3,2,1,0:T(8,128)(2,1)S(1)} %bitcast.2), custom_call_target="tpu_custom_call" | custom-call | tf_op jit(solution)/shard_map/tiles/pallas_call | solution.py:176
Async XLA Ops:
  0.0 3.3 %copy-start.3 = (f32[8,512]{1,0:T(8,128)S(1)}, f32[8,512]{1,0:T(8,128)}, u32[]{:S(2)}) copy-start(f32[8,512]{1,0:T(8,128)} %taps_ref.3) | copy-start | bytes 49156
  0.9 4.9 %collective-permute-start = (bf16[16,3584]{1,0:T(8,128)(2,1)S(1)}, bf16[16,3584]{1,0:T(8,128)(2,1)S(1)}, u32[]{:S(2)}, u32[]{:S(2)}) collective-permute-start(bf16[16,3584]{1,0:T(8,128)(2,1)S(1)} %slice.3), channel_id=1, source_target_pairs={{0,1},{1,2},{2,3},{4,5},{5,6},{6,7},{8,9},{9,10},{10,11},{12,13},{... | collective-permute-start | bytes 344072 | tf_op jit(solution)/shard_map/ppermute | solution.py:192
  3.3 1.2 %copy-start = (bf16[16,32768]{1,0:T(8,128)(2,1)S(1)}, bf16[16,32768]{1,0:T(8,128)(2,1)}, u32[]{:S(2)}) copy-start(bf16[16,32768]{1,0:T(8,128)(2,1)} %head_ref.1) | copy-start | bytes 3145732
  4.6 1.3 %copy-start.1 = (bf16[16,32768]{1,0:T(8,128)(2,1)S(1)}, bf16[16,32768]{1,0:T(8,128)(2,1)}, u32[]{:S(2)}) copy-start(bf16[16,32768]{1,0:T(8,128)(2,1)} %head_ref.1) | copy-start | bytes 3145732
  4.6 1.4 %copy-start.2 = (bf16[512,512]{1,0:T(8,128)(2,1)S(1)}, bf16[512,512]{1,0:T(8,128)(2,1)}, u32[]{:S(2)}) copy-start(bf16[512,512]{1,0:T(8,128)(2,1)} %constant.3.table_ref) | copy-start | bytes 1572868

commit v5 on v4

--- a/solution.py
+++ b/solution.py
@@ -42,9 +42,10 @@
         filt_ref[block // LANES, pl.ds(first + t, xs[0].shape[0], stride=pitch), :] = acc
 
 
-def later_kernel(volts_ref, taps_ref, out_ref, filt_ref):
+def later_kernel(volts_ref, taps_ref, out_ref, head_ref, filt_ref):
     inp, frames = volts_ref.shape[0], volts_ref.shape[1] // FRAME
     pitch = filt_ref.shape[1] // inp
+    head_ref[...] = volts_ref[:, : LEAD * FRAME]
     for block in range(0, FRAME, LANES):
 
         @pl.loop(LEAD // GROUP, frames // GROUP)
@@ -65,9 +66,12 @@
     inp, frames = volts.shape[0], volts.shape[1] // FRAME
     return pl.pallas_call(
         later_kernel,
-        out_shape=jax.ShapeDtypeStruct((inp * frames, FRAME), jnp.bfloat16),
+        out_shape=[
+            jax.ShapeDtypeStruct((inp * frames, FRAME), jnp.bfloat16),
+            jax.ShapeDtypeStruct((inp, LEAD * FRAME), volts.dtype),
+        ],
         in_specs=[VMEM, VMEM],
-        out_specs=VMEM,
+        out_specs=[VMEM, VMEM],
         scratch_shapes=[pltpu.VMEM((FRAME // LANES, inp * (frames + 8), LANES), jnp.float32)],
         compiler_params=params(12),
         cost_estimate=pl.CostEstimate(flops=16 * inp * frames * FRAME, bytes_accessed=1 << 21, transcendentals=0),
@@ -75,13 +79,12 @@
     )(volts, taps)
 
 
-def transform(filtb_ref, table, out_ref, spec_ref, inp):
-    frames = filtb_ref.shape[0] // inp
+def transform(columns, table, out_ref, spec_ref, inp, frames):
     chans = table.shape[0] // 2
     pitch = spec_ref.shape[0] // chans
     low = lax.broadcasted_iota(jnp.int32, (chans, LANES), 1) < frames
     for quad in range(0, inp, WIDE):
-        cols = filtb_ref[quad * frames : (quad + WIDE) * frames, :]
+        cols = jnp.concatenate([columns(i) for i in range(quad, quad + WIDE)], axis=0)
         both = lax.dot_general(table, cols, NT, preferred_element_type=jnp.float32)
         for p in range(WIDE // 2):
             real, imag = (both[c * chans : (c + 1) * chans, p * LANES : (p + 1) * LANES] for c in (0, 1))
@@ -92,49 +95,48 @@
         out_ref[k * inp : (k + 1) * inp, :] = spec_ref[k * pitch : k * pitch + inp, :].astype(jnp.bfloat16)
 
 
-def front_kernel(later_ref, halo_ref, head_ref, taps_ref, table_ref, out_ref, filtb_ref, filt_ref, spec_ref, sem):
+def front_kernel(later_ref, halo_ref, head_ref, taps_ref, table_ref, out_ref, filt_ref, spec_ref):
     inp = head_ref.shape[0]
-    frames = filtb_ref.shape[0] // inp
-    copy = pltpu.make_async_copy(later_ref, filtb_ref, sem)
-    copy.start()
+    frames = later_ref.shape[0] // inp
+    pitch = filt_ref.shape[1] // inp
+    follows = lax.axis_index("tm") > 0
     for block in range(0, FRAME, LANES):
         for first in range(0, LEAD, GROUP):
 
             def slab(g):
                 t = first + g - (TAPS - 1)
                 ref, at = (halo_ref, t + TAPS - 1) if t < 0 else (head_ref, t)
-                return ref[:, at * FRAME + block : at * FRAME + block + LANES].astype(jnp.float32)
-
-            filter_group(slab, first, block, taps_ref, filt_ref, filt_ref.shape[1] // inp)
-    copy.wait()
-    pitch = filt_ref.shape[1] // inp
-    for block in range(0, FRAME, LANES):
-        for i in range(inp):
-            filtb_ref[i * frames : i * frames + LEAD, block : block + LANES] = filt_ref[
-                block // LANES, i * pitch : i * pitch + LEAD, :
-            ].astype(jnp.bfloat16)
-    transform(filtb_ref, table_ref[...], out_ref, spec_ref, inp)
-
-
-def front(filtered, halo, volts, taps, table):
-    inp = volts.shape[0]
-    frames = volts.shape[1] // FRAME
+                held = ref[:, at * FRAME + block : at * FRAME + block + LANES].astype(jnp.float32)
+                return held if t >= 0 else jnp.where(follows, held, 0.0)
+
+            filter_group(slab, first, block, taps_ref, filt_ref, pitch)
+
+    def columns(i):
+        lead = [filt_ref[b, i * pitch : i * pitch + LEAD, :].astype(jnp.bfloat16) for b in range(FRAME // LANES)]
+        return jnp.concatenate(
+            [jnp.concatenate(lead, axis=1), later_ref[i * frames + LEAD : (i + 1) * frames, :]], axis=0
+        )
+
+    transform(columns, table_ref[...], out_ref, spec_ref, inp, frames)
+
+
+def front(filtered, halo, head, taps, table):
+    inp = head.shape[0]
+    frames = filtered.shape[0] // inp
     assert 2 * frames == LANES
     chans = table.shape[0] // 2
     return pl.pallas_call(
         front_kernel,
         out_shape=jax.ShapeDtypeStruct((chans * inp, LANES), jnp.bfloat16),
-        in_specs=[ANY, VMEM, VMEM, VMEM, VMEM],
+        in_specs=[VMEM] * 5,
         out_specs=VMEM,
         scratch_shapes=[
-            pltpu.VMEM(filtered.shape, jnp.bfloat16),
             pltpu.VMEM((FRAME // LANES, inp * (LEAD + 8), LANES), jnp.float32),
             pltpu.VMEM((chans * (inp + 8), LANES), jnp.float32),
-            pltpu.SemaphoreType.DMA,
         ],
         compiler_params=params(16),
         name="front",
-    )(filtered, halo, volts, taps, table)
+    )(filtered, halo, head, taps, table)
 
 
 def tiles_kernel(groups, blocks_time, scale, spec_ref, out_ref, held_ref, sem):
@@ -189,9 +191,9 @@
     frames = voltages.shape[1] // FRAME
     groups, blocks_time = lax.axis_size("inputs"), lax.axis_size("tm")
     tail = voltages[:, voltages.shape[1] - (TAPS - 1) * FRAME :]
-    halo = lax.ppermute(tail, "tm", [(i, i + 1) for i in range(blocks_time - 1)])
-    filtered = later(voltages, pfb_taps)
-    spec = front(filtered, halo, voltages, pfb_taps, dft_table(F, FRAME))
+    halo = lax.ppermute(tail, "tm", [(i, (i + 1) % blocks_time) for i in range(blocks_time)])
+    filtered, head = later(voltages, pfb_taps)
+    spec = front(filtered, halo, head, pfb_taps, dft_table(F, FRAME))
     turned = lax.all_to_all(spec, ("inputs", "tm"), split_axis=0, concat_axis=0, tiled=True)
     scale = 1.0 / (frames * blocks_time)
     every = groups * blocks_time

time: 43.5 us -> 41.3 us (0.949)
  starting transfers between devices: 2.39 us -> 0.49 us
  waiting for transfers between devices: 0.01 us -> 1.89 us
  blocking collectives: 34.5 us -> 32.7 us
    ppermute x1, starting transfers between devices: 2.39 us -> 0.49 us  [on_device(): lax.ppermute(tail, 'tm', [(i, (i + 1) % blocks_time) for i in range(block...]
    ppermute x1, waiting for transfers between devices: 0.01 us -> 1.89 us  [on_device(): lax.ppermute(tail, 'tm', [(i, (i + 1) % blocks_time) for i in range(block...]
    all_to_all x1, blocking collectives: 34.5 us -> 32.7 us  [on_device(): lax.all_to_all(spec, ('inputs', 'tm'), split_axis=0, concat_axis=0, tiled...]
    unnamed x8 -> x6, local copies, waits for them, and re-layouts: 1.31 us -> 1.23 us
  transfers between devices with their start and end apart: 1 -> 1, of which waited for: 0 -> 1; matrix products, arithmetic and copies ran while one was open for 0% -> 0% of each run, Pallas kernels for 3% -> 3%
where the time goes in v5:
time: 41.3 us; the launch traced here: 41.1 us
  blocking collectives  32.7 us (79%)
  Pallas kernels  3.9 us (9%)
  local copies, waits for them, and re-layouts  2.15 us (5%)
  waiting for transfers between devices  1.89 us (5%)
  starting transfers between devices  0.49 us (1%)
    all_to_all x1, blocking collectives, on_device(): lax.all_to_all(spec, ('inputs', 'tm'), split_axis=0, concat_axis=0, tiled...  32.7 us
    ppermute x1, waiting for transfers between devices, on_device(): lax.ppermute(tail, 'tm', [(i, (i + 1) % blocks_time) for i in range(block...  1.89 us
    pallas_call x1, Pallas kernels, tile_sums(): pl.pallas_call(functools.partial(tiles_kernel, groups, blocks_time, scale...  1.46 us
    pallas_call x1, Pallas kernels, later(): pl.pallas_call(later_kernel, out_shape=[jax.ShapeDtypeStruct((inp * frame...  1.26 us
    unnamed x6, local copies, waits for them, and re-layouts  1.23 us
    pallas_call x1, Pallas kernels, front(): pl.pallas_call(front_kernel, out_shape=jax.ShapeDtypeStruct((chans * inp,...  1.17 us
    slice x1, local copies, waits for them, and re-layouts, on_device(): tail = voltages[:, voltages.shape[1] - (TAPS - 1) * FRAME:]  0.92 us
  transfers between devices with their start and end apart: 1, of which 1 were waited for; matrix products, arithmetic and copies ran while one was open for 0% of the time, Pallas kernels for 3%

profile of v5, /device:TPU:0, one launch (start us, length us, event | category | flops | bytes accessed | tf_op | source)
XLA Modules:
  0.0 41.1 jit_solution(13802552089688792269)
XLA Ops:
  0.0 0.0 copy-start.2
  0.0 0.9 %slice.3 = bf16[16,3584]{1,0:T(8,128)(2,1)S(1)} slice(bf16[16,32768]{1,0:T(8,128)(2,1)} %volts_ref.1), slice={[0:16], [29184:32768]} | slice | bytes 229376 | tf_op jit(solution)/shard_map/slice | solution.py:193
  0.9 0.5 %collective-permute-start = (bf16[16,3584]{1,0:T(8,128)(2,1)S(1)}, bf16[16,3584]{1,0:T(8,128)(2,1)S(1)}, u32[]{:S(2)}, u32[]{:S(2)}) collective-permute-start(bf16[16,3584]{1,0:T(8,128)(2,1)S(1)} %slice.3), channel_id=1, source_target_pairs={{0,1},{1,2},{2,3},{3,0},{4,5},{5,6},{6,7},{7,4},{8,9},{9,10},{10,1... | collective-permute-start | bytes 344072 | tf_op jit(solution)/shard_map/ppermute | solution.py:194
  1.4 0.0 copy-done.2
  1.4 0.0 copy-start
  1.4 1.2 %copy-done = bf16[16,32768]{1,0:T(8,128)(2,1)S(1)} copy-done((bf16[16,32768]{1,0:T(8,128)(2,1)S(1)}, bf16[16,32768]{1,0:T(8,128)(2,1)}, u32[]{:S(2)}) %copy-start) | copy-done | bytes 1048600
  2.6 0.0 copy-start.1
  2.6 1.3 %later.1 = (bf16[1024,512]{1,0:T(8,128)(2,1)S(1)}, bf16[16,8192]{1,0:T(8,128)(2,1)S(1)}) custom-call(bf16[16,32768]{1,0:T(8,128)(2,1)S(1)} %copy-done, f32[8,512]{1,0:T(8,128)S(1)} %copy-done.2), custom_call_target="tpu_custom_call" | custom-call | flops 8388608 | bytes 2097152 | tf_op jit(solution)/shard_map/later/pallas_call | solution.py:67
  3.9 1.9 %collective-permute-done.halo_ref = bf16[16,3584]{1,0:T(8,128)(2,1)S(1)} collective-permute-done((bf16[16,3584]{1,0:T(8,128)(2,1)S(1)}, bf16[16,3584]{1,0:T(8,128)(2,1)S(1)}, u32[]{:S(2)}, u32[]{:S(2)}) %collective-permute-start) | collective-permute-done | bytes 114720 | tf_op jit(solution)/shard_map/ppermute | solution.py:194
  5.8 0.0 copy-done.1
  5.8 1.2 %front.1 = bf16[4096,128]{1,0:T(8,128)(2,1)S(1)} custom-call(bf16[1024,512]{1,0:T(8,128)(2,1)S(1)} %get-tuple-element.7.later_ref, bf16[16,3584]{1,0:T(8,128)(2,1)S(1)} %collective-permute-done.halo_ref, bf16[16,8192]{1,0:T(8,128)(2,1)S(1)} %get-tuple-element.8.head_ref, f32[8,512]{1,0:T(8,128)S(1)} %copy-done.2, bf16[512,512]{1,0:T(8,128)(2,1)S(1)} %copy-done.1), custom_call_target="tpu_custom_call" | custom-call | tf_op jit(solution)/shard_map/front/pallas_call | solution.py:128
  7.0 32.7 %all_to_all.9 = bf16[32,128,128]{2,1,0:T(8,128)(2,1)S(1)} all-to-all(bf16[32,128,128]{2,1,0:T(8,128)(2,1)S(1)} %bitcast.2), channel_id=1, replica_groups=mesh['inputs'=8,'tm'=4] {'inputs','tm'}, dimensions={0} | all-to-all | bytes 2097152 | tf_op jit(solution)/shard_map/all_to_all | solution.py:197
  39.7 1.5 %tiles.1 = f32[8,1,2,128,128]{4,3,2,1,0:T(8,128)} custom-call(bf16[32,8,16,128]{3,2,1,0:T(8,128)(2,1)S(1)} %bitcast.3), custom_call_target="tpu_custom_call" | custom-call | tf_op jit(solution)/shard_map/tiles/pallas_call | solution.py:178
Async XLA Ops:
  0.0 1.4 %copy-start.2 = (f32[8,512]{1,0:T(8,128)S(1)}, f32[8,512]{1,0:T(8,128)}, u32[]{:S(2)}) copy-start(f32[8,512]{1,0:T(8,128)} %taps_ref.3) | copy-start | bytes 49156
  0.9 4.9 %collective-permute-start = (bf16[16,3584]{1,0:T(8,128)(2,1)S(1)}, bf16[16,3584]{1,0:T(8,128)(2,1)S(1)}, u32[]{:S(2)}, u32[]{:S(2)}) collective-permute-start(bf16[16,3584]{1,0:T(8,128)(2,1)S(1)} %slice.3), channel_id=1, source_target_pairs={{0,1},{1,2},{2,3},{3,0},{4,5},{5,6},{6,7},{7,4},{8,9},{9,10},{10,1... | collective-permute-start | bytes 344072 | tf_op jit(solution)/shard_map/ppermute | solution.py:194
  1.4 1.2 %copy-start = (bf16[16,32768]{1,0:T(8,128)(2,1)S(1)}, bf16[16,32768]{1,0:T(8,128)(2,1)}, u32[]{:S(2)}) copy-start(bf16[16,32768]{1,0:T(8,128)(2,1)} %volts_ref.1) | copy-start | bytes 3145732
  2.6 3.2 %copy-start.1 = (bf16[512,512]{1,0:T(8,128)(2,1)S(1)}, bf16[512,512]{1,0:T(8,128)(2,1)}, u32[]{:S(2)}) copy-start(bf16[512,512]{1,0:T(8,128)(2,1)} %constant.3.table_ref) | copy-start | bytes 1572868
